TPU v7x, 512 devices: a whole 4x8x8 slice. The times are simulated.
512 devices in a mesh: left: 16 (over x, y_hi, core), right: 32 (over y_lo, z).
Axes of the slice: x: 4, y: 8 (y_hi: 2, y_lo: 4; y = y_hi * 4 + y_lo), z: 8, core: 2. Of those that a mesh axis runs over, the one named last changes fastest.
Arguments:
- left_table: bfloat16 [32768, 256], P('left'), may hold values from -1.5 to 1.5
- right_table: bfloat16 [16, 16384, 256], P('left', 'right'), may hold values from -1.5 to 1.5
- relations: float32 [512, 256], replicated, may hold values from -6 to 6
- source_ids: int32 [16, 32, 1024], P('left', 'right'), may hold values from 0 to 2047
- relation_ids: int32 [16, 32, 1024], P('left', 'right'), may hold values from 0 to 511
- target_ids: int32 [16, 32, 1024], P('left', 'right'), may hold values from 0 to 511
- negative_ids: int32 [16, 32, 1, 1024], P('left', 'right'), may hold values from 0 to 511
- edge_counts: int32 [16, 32], P('left', 'right'), may hold values from 1 to 1024
Outputs:
- left_next: bfloat16 [32768, 256], P('left')
- right_next: bfloat16 [16, 16384, 256], P('left', 'right')
- relations_next: float32 [512, 256], replicated
Inputs may be any that keep to these rules, and one draw needn't show every extreme that they name: Edge slots at positions from edge_counts to 1023 hold ids but are padding.
All inputs are finite; a program needn't handle non-finite values.
Results may differ from a plain program's by a relative error of at most 0.0013.
Values may be sent and summed in bfloat16 or wider, within the bound.
No kernel may reach another device: no remote copies, remote signals or barrier semaphores. Data moves between devices by JAX's collectives and lax.ppermute only.
A program may use at most 64 MiB of HBM per device.

v0:
```python
import jax
import jax.numpy as jnp
from jax import lax
from jax.sharding import PartitionSpec as P

step_size = 0.5
relation_step = 12.0


def passed_along(array, axis, by):
    peers = lax.axis_size(axis)
    return lax.ppermute(array, axis, [(i, (i + by) % peers) for i in range(peers)])


def block_terms(left_blk, right_blk, relations, src, kind, dst, neg, live):
    half = relations.shape[1] // 2
    head = jnp.take(left_blk, src, axis=0).astype(jnp.float32)
    tail = jnp.take(right_blk, dst, axis=0).astype(jnp.float32)
    rel = jnp.take(relations, kind, axis=0)
    hre, him = (head[:, :half], head[:, half:])
    rre, rim = (rel[:, :half], rel[:, half:])
    query = jnp.concatenate([hre * rre - him * rim, hre * rim + him * rre], axis=1)
    q_low = query.astype(jnp.bfloat16)
    pos = jnp.sum(query * tail, axis=1)
    negrows = jnp.take(right_blk, neg, axis=0)
    scores = lax.dot_general(
        q_low, negrows, (((1,), (1,)), ((), ())), preferred_element_type=jnp.float32
    )
    c_pos = -jax.nn.sigmoid(-pos) * live
    c_neg = (jax.nn.sigmoid(scores) * (live[:, None] / neg.shape[0])).astype(jnp.bfloat16)
    g_query = jnp.dot(c_neg, negrows, preferred_element_type=jnp.float32) + c_pos[:, None] * tail
    g_neg = lax.dot_general(
        c_neg, q_low, (((0,), (0,)), ((), ())), preferred_element_type=jnp.float32
    )
    g_tail = c_pos[:, None] * query
    gre, gim = (g_query[:, :half], g_query[:, half:])
    grad_h = jnp.concatenate([gre * rre + gim * rim, -gre * rim + gim * rre], axis=1)
    grad_r = jnp.concatenate([gre * hre + gim * him, -gre * him + gim * hre], axis=1)
    return (grad_h, grad_r, g_tail, g_neg)


def shards(
    left_table,
    right_table,
    relations,
    source_ids,
    relation_ids,
    target_ids,
    negative_ids,
    edge_counts,
):
    right_blk = right_table[0]
    src_all = source_ids[0, 0]
    kind_all = relation_ids[0, 0]
    dst_all = target_ids[0, 0]
    negs = negative_ids[0, 0]
    count = edge_counts[0, 0]
    blocks = negs.shape[0]
    width = src_all.shape[0] // blocks
    live_blocks = (count + width - 1) // width

    def one(index, carry):
        lgrad, rgrad, tgrad = carry
        start = index * width
        n = lax.dynamic_index_in_dim(negs, index, 0, keepdims=False)
        live = (start + jnp.arange(width, dtype=jnp.int32) < count).astype(jnp.float32)
        grad_h, grad_r, g_tail, g_neg = block_terms(
            left_table, right_blk, relations, src_all, kind_all, dst_all, n, live
        )
        lgrad = lgrad.at[src_all].add(grad_h)
        rgrad = rgrad.at[kind_all].add(grad_r)
        tgrad = tgrad.at[dst_all].add(g_tail).at[n].add(g_neg)
        return (lgrad, rgrad, tgrad)

    init = (
        jnp.zeros(left_table.shape, jnp.float32),
        jnp.zeros(relations.shape, jnp.float32),
        jnp.zeros(right_blk.shape, jnp.float32),
    )
    left_grad, rel_grad, right_grad = lax.fori_loop(0, live_blocks, one, init)
    updated = (right_blk.astype(jnp.float32) - step_size * right_grad).astype(jnp.bfloat16)
    moved = passed_along(updated, "right", 1)
    left_total = lax.psum(left_grad, "right")
    rel_total = lax.psum(rel_grad, ("left", "right"))
    left_next = (left_table.astype(jnp.float32) - step_size * left_total).astype(jnp.bfloat16)
    relations_next = relations - relation_step * rel_total
    return (left_next, moved[None], relations_next)


def solution(mesh):
    return jax.shard_map(
        shards,
        mesh=mesh,
        in_specs=(
            P("left", None),
            P("left", "right", None),
            P(),
            P("left", "right", None),
            P("left", "right", None),
            P("left", "right", None),
            P("left", "right", None, None),
            P("left", "right"),
        ),
        out_specs=(P("left", None), P("left", "right", None), P()),
        check_vma=False,
    )
```

profile of v0, /device:TPU:2, one launch (start us, length us, event | category | flops | bytes accessed | tf_op | source)
XLA Modules:
  0.0 709.8 jit_solution(15141002125790694229)
XLA Ops:
  7.9 0.7 compare_and_fusion.4
  8.6 0.7 fusion.13
  9.2 0.7 compare_select_fusion.9
  9.9 0.7 compare_and_fusion.6
  10.6 0.7 compare_select_fusion.8
  11.3 0.7 compare_and_fusion.5
  12.0 4.9 gather_fusion.4
  16.9 3.9 gather_fusion.6
  20.9 0.2 select_convert_fusion.1
  21.1 3.5 gather_fusion.5
  25.0 0.4 fusion.12
  25.5 1.4 broadcast_in_dim.66
  26.9 80.2 %while.17 = (s32[]{:T(128)}, f32[2048,256]{1,0:T(8,128)}, f32[512,256]{1,0:T(8,128)S(1)}, f32[512,256]{1,0:T(8,128)S(1)}, s32[]{:T(128)}, /*index=5*/s32[1024]{0...) while((s32[]{:T(128)}, f32[2048,256]{1,0:T(8,128)}, ...), condition=%wide.region_6.8_spmd, body=%wide.region_1.7_spmd.sunk | while | flops 1624953856 | bytes 75646288 | solution.py:80
  27.3 0.7 negate_select_fusion.2
  28.0 5.0 gather_fusion
  32.9 3.9 gather_fusion.3
  36.9 1.0 copy.28
  37.9 5.0 gather_fusion.2
  42.9 1.2 copy.27
  44.1 1.0 select_convert_fusion.3
  45.2 4.7 gather_fusion.1
  49.8 2.6 copy.26
  52.4 1.4 broadcast_select_fusion.10
  54.0 0.2 multiply_subtract_fusion.4
  54.2 0.8 copy-done.5
  55.0 0.8 copy-done.6
  55.8 1.1 fusion.30
  56.9 2.5 copy.31
  59.4 6.7 scatter_fusion.2
  66.2 3.0 multiply_convert_fusion.2
  69.2 1.8 convolution_add_fusion.2
  71.0 1.8 fusion.31
  72.8 6.7 scatter_fusion.3
  79.5 3.0 multiply_add_fusion.7
  82.6 1.0 pad_maximum_fusion.5
  83.6 2.5 copy.29
  86.1 9.4 %scatter_fusion = f32[2048,256]{1,0:T(8,128)} fusion(f32[2048,256]{1,0:T(8,128)} %get-tuple-element.393, s32[1024]{0:T(1024)S(1)} %bitcast.59, f32[1024,256]{1,0:T(8,128)} %copy.29), kind=kCustom, calls=%fused_computation.7.clone.1 | custom fusion | flops 262144 | bytes 3149824 | tf_op jit(solution)/shard_map/while/body/scatter-add | solution.py:70
  95.5 2.1 pad_maximum_fusion.6
  97.6 2.5 copy.30
  100.1 6.7 scatter_fusion.1
  107.1 0.8 copy-done.2
  108.0 0.7 all-reduce.3.cloned.1.call-update
  108.8 4.3 collective-permute-start
  113.0 270.8 %all-reduce.5.cloned.1.call-done = f32[512,256]{1,0:T(8,128)} async-done(((f32[512,256]{1,0:T(8,128)}), f32[512,256]{1,0:T(8,128)}) %all-reduce.5.cloned.1.call-update) | async-done | bytes 524304 | tf_op jit(solution)/shard_map/psum | solution.py:84
  383.8 1.9 multiply_subtract_fusion.1
  385.7 313.7 %all-reduce.3.cloned.1.call-done = f32[2048,256]{1,0:T(8,128)} async-done(((f32[2048,256]{1,0:T(8,128)}), f32[2048,256]{1,0:T(8,128)}) %all-reduce.3.cloned.1.call-update) | async-done | bytes 2097168 | tf_op jit(solution)/shard_map/psum | solution.py:83
  699.4 2.8 subtract_convert_fusion
  702.2 0.7 copy.54
  (48 shorter events, 0.8 us)
Async XLA Ops:
  7.2 376.7 %all-reduce.5.cloned.1.call-start = ((), (), s32[]{:S(2)}) async-start(), calls=%async_computation.1 | async-start | bytes 1048576 | tf_op jit(solution)/shard_map/psum | solution.py:84
  12.0 4.9 copy-start
  16.9 4.2 copy-start.1
  24.9 2.0 copy-start.3
  24.9 2.0 copy-start.10
  24.9 2.0 copy-start.11
  25.0 2.0 copy-start.12
  25.0 2.0 copy-start.13
  52.4 1.5 copy-start.4
  54.0 1.0 copy-start.5
  55.0 0.8 copy-start.6
  66.2 3.0 copy-start.8
  66.2 3.0 copy-start.9
  69.2 1.8 copy-start.7
  107.1 0.8 copy-start.2
  107.9 591.5 %all-reduce.3.cloned.1.call-start = ((), (), s32[]{:S(2)}) async-start(), calls=%async_computation | async-start | bytes 4194304 | tf_op jit(solution)/shard_map/psum | solution.py:83
  108.8 277.0 %collective-permute-start = (bf16[512,256]{1,0:T(8,128)(2,1)S(1)}, bf16[512,256]{1,0:T(8,128)(2,1)S(1)}, u32[]{:S(2)}, u32[]{:S(2)}) collective-permute-start(bf16[512,256]{1,0:T(8,128)(2,1)S(1)} %subtract_convert_fusion.1), channel_id=1, source_target_pairs={{0,1},{1,2},{2,3},{3,4},{4,5},{5,6},{6,7},{7,8},{8,9},{9,10},{10,1... | collective-permute-start | bytes 786440 | tf_op jit(solution)/shard_map/ppermute | solution.py:12
Sparse Core Ops, SparseCore 0:
  108.1 275.7 all-reduce.4
  386.7 312.6 all-reduce.2
where the time goes:
time: 711 us; the launch traced here: 710 us
  waiting for transfers between devices  585 us (82%)
  other arithmetic  50.1 us (7%)
  local copies, waits for them, and re-layouts  48.1 us (7%)
  between operations  14.9 us (2%)
    psum x1, waiting for transfers between devices, shards(): left_total = lax.psum(left_grad, 'right')  314 us
    psum x1, waiting for transfers between devices, shards(): rel_total = lax.psum(rel_grad, ('left', 'right'))  271 us
  transfers between devices with their start and end apart: 3, of which 2 were waited for; matrix products, arithmetic and copies ran while one was open for 0% of the time, Pallas kernels for 0%

commit v1 on v0

--- a/solution.py
+++ b/solution.py
@@ -81,7 +81,9 @@
     updated = (right_blk.astype(jnp.float32) - step_size * right_grad).astype(jnp.bfloat16)
     moved = passed_along(updated, "right", 1)
     left_total = lax.psum(left_grad, "right")
-    rel_total = lax.psum(rel_grad, ("left", "right"))
+    rel_total = rel_grad
+    for j in ("left", "right"):
+        rel_total = lax.psum(rel_total, axis_name=j)
     left_next = (left_table.astype(jnp.float32) - step_size * left_total).astype(jnp.bfloat16)
     relations_next = relations - relation_step * rel_total
     return (left_next, moved[None], relations_next)

time: 711 us -> 630 us (0.89)
  waiting for transfers between devices: 585 us -> 507 us
    psum x1, waiting for transfers between devices: 271 us -> 180 us  [shards(): rel_total = lax.psum(rel_total, axis_name=j)]
    ppermute x1, waiting for transfers between devices: 0.01 us -> 10.8 us  [passed_along(): lax.ppermute(array, axis, [(i, (i + by) % peers) for i in range(peers)])]
  transfers between devices with their start and end apart: 3 -> 3, of which waited for: 2 -> 3; matrix products, arithmetic and copies ran while one was open for 0% -> 0% of each run, Pallas kernels for 0% -> 0%
where the time goes in v1:
time: 630 us; the launch traced here: 629 us
  waiting for transfers between devices  507 us (80%)
  other arithmetic  49.1 us (8%)
  local copies, waits for them, and re-layouts  48 us (8%)
  between operations  14.9 us (2%)
  matrix products  6.52 us (1%)
    psum x1, waiting for transfers between devices, shards(): left_total = lax.psum(left_grad, 'right')  316 us
    psum x1, waiting for transfers between devices, shards(): rel_total = lax.psum(rel_total, axis_name=j)  180 us
    scatter-add x2, other arithmetic, one(): tgrad = tgrad.at[dst_all].add(g_tail).at[n].add(g_neg)  13.5 us
  transfers between devices with their start and end apart: 3, of which 3 were waited for; matrix products, arithmetic and copies ran while one was open for 0% of the time, Pallas kernels for 0%

profile of v1, /device:TPU:2, one launch (start us, length us, event | category | flops | bytes accessed | tf_op | source)
XLA Modules:
  0.0 629.5 jit_solution(2600665460816306039)
XLA Ops:
  7.9 0.7 compare_and_fusion.4
  8.6 0.7 fusion.13
  9.2 0.7 compare_select_fusion.9
  9.9 0.7 compare_and_fusion.6
  10.6 0.7 compare_select_fusion.8
  11.3 0.7 compare_and_fusion.5
  12.0 4.9 gather_fusion.4
  16.9 3.9 gather_fusion.6
  20.9 0.2 select_convert_fusion.1
  21.1 3.5 gather_fusion.5
  25.0 0.4 fusion.12
  25.5 1.5 broadcast_in_dim.66
  26.9 80.1 %while.17 = (s32[]{:T(128)}, f32[2048,256]{1,0:T(8,128)}, f32[512,256]{1,0:T(8,128)S(1)}, f32[512,256]{1,0:T(8,128)S(1)}, s32[]{:T(128)}, /*index=5*/s32[1024]{0...) while((s32[]{:T(128)}, f32[2048,256]{1,0:T(8,128)}, ...), condition=%wide.region_6.8_spmd, body=%wide.region_1.7_spmd.sunk | while | flops 1624953856 | bytes 75646288 | solution.py:80
  27.3 0.7 negate_select_fusion.2
  28.0 5.0 gather_fusion
  32.9 3.9 gather_fusion.3
  36.9 1.0 copy.28
  37.9 5.0 gather_fusion.2
  42.9 1.2 copy.27
  44.1 1.0 select_convert_fusion.3
  45.2 4.7 gather_fusion.1
  49.9 2.6 copy.26
  52.4 1.4 broadcast_select_fusion.10
  54.0 0.2 multiply_subtract_fusion.4
  54.2 0.8 copy-done.5
  55.0 0.8 copy-done.6
  55.8 1.1 fusion.30
  56.9 2.5 copy.31
  59.4 6.7 %scatter_fusion.2 = f32[512,256]{1,0:T(8,128)S(1)} fusion(f32[512,256]{1,0:T(8,128)S(1)} %get-tuple-element.397, s32[1024]{0:T(1024)S(1)} %bitcast.70, f32[1024,256]{1,0:T(8,128)} %copy.31), kind=kCustom, calls=%fused_computation.9.clone.1 | custom fusion | flops 262144 | bytes 3149824 | tf_op jit(solution)/shard_map/while/body/scatter-add | solution.py:72
  66.2 3.0 multiply_convert_fusion.2
  69.2 1.8 convolution_add_fusion.2
  71.0 1.7 fusion.31
  72.7 6.7 %scatter_fusion.3 = f32[512,256]{1,0:T(8,128)S(1)} fusion(f32[512,256]{1,0:T(8,128)S(1)} %scatter_fusion.2, s32[1024]{0:T(1024)S(1)} %bitcast.69, f32[1024,256]{1,0:T(8,128)} %fusion.31), kind=kCustom, calls=%fused_computation.10.clone.1 | custom fusion | flops 262144 | bytes 3149824 | tf_op jit(solution)/shard_map/while/body/scatter-add | solution.py:72
  79.5 3.0 multiply_add_fusion.7
  82.5 1.0 pad_maximum_fusion.5
  83.5 2.5 copy.29
  86.0 9.4 %scatter_fusion = f32[2048,256]{1,0:T(8,128)} fusion(f32[2048,256]{1,0:T(8,128)} %get-tuple-element.395, s32[1024]{0:T(1024)S(1)} %bitcast.59, f32[1024,256]{1,0:T(8,128)} %copy.29), kind=kCustom, calls=%fused_computation.7.clone.1 | custom fusion | flops 262144 | bytes 3149824 | tf_op jit(solution)/shard_map/while/body/scatter-add | solution.py:70
  95.4 2.1 pad_maximum_fusion.6
  97.5 2.5 copy.30
  100.1 6.7 %scatter_fusion.1 = f32[512,256]{1,0:T(8,128)S(1)} fusion(f32[512,256]{1,0:T(8,128)S(1)} %get-tuple-element.396, s32[1024]{0:T(1024)S(1)} %bitcast.57, f32[1024,256]{1,0:T(8,128)} %copy.30), kind=kCustom, calls=%fused_computation.8.clone.1 | custom fusion | flops 262144 | bytes 3149824 | tf_op jit(solution)/shard_map/while/body/scatter-add | solution.py:71
  107.1 0.8 copy-done.2
  107.9 180.2 %all-reduce.4.cloned.1.call-done = f32[512,256]{1,0:T(8,128)} async-done(((f32[512,256]{1,0:T(8,128)}), f32[512,256]{1,0:T(8,128)}) %all-reduce.4.cloned.1.call-update) | async-done | bytes 524304 | tf_op jit(solution)/shard_map/psum | solution.py:86
  288.2 3.1 collective-permute-start
  291.4 10.8 %collective-permute-done = bf16[512,256]{1,0:T(8,128)(2,1)S(1)} collective-permute-done((bf16[512,256]{1,0:T(8,128)(2,1)S(1)}, bf16[512,256]{1,0:T(8,128)(2,1)S(1)}, u32[]{:S(2)}, u32[]{:S(2)}) %collective-permute-start) | collective-permute-done | bytes 262176 | tf_op jit(solution)/shard_map/ppermute | solution.py:12
  302.1 316.0 %all-reduce.6.cloned.1.call-done = (f32[2048,256]{1,0:T(8,128)}, f32[512,256]{1,0:T(8,128)}) async-done(((f32[2048,256]{1,0:T(8,128)}, f32[512,256]{1,0:T(8,128)}), (f32[2048,256]{1,0:T(8,128)}, f32[512,256]{1,0:T(8,128)})) %all-reduce.6.cloned.1.call-update) | async-done | bytes 2621456 | tf_op jit(solution)/shard_map/psum | solution.py:83
  618.2 2.9 subtract_convert_fusion
  621.0 0.9 multiply_subtract_fusion.1
  621.9 0.7 copy.55
  (50 shorter events, 0.9 us)
Async XLA Ops:
  7.2 281.0 %all-reduce.4.cloned.1.call-start = ((), (), s32[]{:S(2)}) async-start(), calls=%async_computation | async-start | bytes 1048576 | tf_op jit(solution)/shard_map/psum | solution.py:86
  12.0 4.9 copy-start
  16.9 4.2 copy-start.1
  24.9 2.0 copy-start.3
  24.9 2.0 copy-start.10
  24.9 2.0 copy-start.11
  25.0 2.0 copy-start.12
  25.0 2.0 copy-start.13
  52.4 1.5 copy-start.4
  54.0 1.0 copy-start.5
  55.0 0.8 copy-start.6
  66.1 3.0 copy-start.8
  66.2 3.0 copy-start.9
  69.2 1.8 copy-start.7
  107.0 0.8 copy-start.2
  107.9 510.3 %all-reduce.6.cloned.1.call-start = ((), (), s32[]{:S(2)}) async-start(), calls=%async_computation.1 | async-start | bytes 5242880 | tf_op jit(solution)/shard_map/psum | solution.py:83
  288.2 13.9 %collective-permute-start = (bf16[512,256]{1,0:T(8,128)(2,1)S(1)}, bf16[512,256]{1,0:T(8,128)(2,1)S(1)}, u32[]{:S(2)}, u32[]{:S(2)}) collective-permute-start(bf16[512,256]{1,0:T(8,128)(2,1)S(1)} %subtract_convert_fusion.1), channel_id=1, source_target_pairs={{0,1},{1,2},{2,3},{3,4},{4,5},{5,6},{6,7},{7,8},{8,9},{9,10},{10,1... | collective-permute-start | bytes 786440 | tf_op jit(solution)/shard_map/ppermute | solution.py:12
  618.2 2.9 copy-start.14
Sparse Core Ops, SparseCore 0:
  108.0 180.1 all-reduce.3
  291.1 326.9 all-reduce.5
